TPU v7x, 256 devices: a whole 4x4x8 slice. The times are simulated.
256 devices in a mesh: leaf: 32 (over x, y, core), front: 8 (over z).
Axes of the slice: x: 4, y: 4, z: 8, core: 2. Of those that a mesh axis runs over, the one named last changes fastest.
Arguments:
- child_updates: float32 [32768, 1024], P('leaf', 'front'), as said below
- initial_one: float32 [32768, 2048], P('leaf', 'front'), as said below
- initial_two: float32 [16384, 2048], P('leaf', 'front'), as said below
- pattern_one: int32 [16, 16, 16], replicated, may hold values 0 or 1
- pattern_two: int32 [8, 16, 16], replicated, may hold values 0 or 1
- parent_map_one: int32 [16, 2, 16], replicated, may hold values from 0 to 15, each once within a row
- parent_map_two: int32 [8, 2, 16], replicated, may hold values from 0 to 15, each once within a row
Outputs:
- factor_one: float32 [32768, 1024], P('leaf', 'front')
- factor_two: float32 [16384, 1024], P('leaf', 'front')
- schur_two: float32 [8192, 1024], P('leaf', 'front')
Inputs may be any that keep to these rules, and one draw needn't show every extreme that they name: `parent_map_one`: each row is a permutation of 0 to 15; only its first 8 entries are used. `parent_map_two`: each row is a permutation of 0 to 15; only its first 8 entries are used. `initial_one`: each 2048 x 2048 front block is symmetric, and positive definite after any symmetric block mask. `initial_two`: each 2048 x 2048 front block is symmetric, and positive definite after any symmetric block mask. `child_updates`: each 1024 x 1024 matrix is symmetric positive definite.
All inputs are finite; a program needn't handle non-finite values.
Results may differ from a plain program's by a relative error of at most 0.0003.
Values sent between devices are 32-bit elements; how exact they have to be, the bound alone decides.
No kernel may reach another device: no remote copies, remote signals or barrier semaphores. Data moves between devices by JAX's collectives and lax.ppermute only.
A program may use at most 128 MiB of HBM per device.

v0:
```python
import jax
import jax.numpy as jnp
from jax import lax
from jax.sharding import PartitionSpec as P

BLK = 128
SEP = 1024
UPD = 1024
FR = 2048


HIGHEST = lax.Precision.HIGHEST


def swapped(block, axis, stride):
    count = lax.axis_size(axis)
    route = []
    for low in range(count):
        high = low | 1 << stride
        if high != low and high < count:
            route += [(low, high), (high, low)]
    return lax.ppermute(block, axis, route)


def spread(block, axis, holder):
    block = jnp.where(lax.axis_index(axis) == holder, block, jnp.zeros_like(block))
    return lax.psum(block, axis)


def solve_rows(chol_block, right_side):
    return jax.scipy.linalg.solve_triangular(chol_block, right_side.T, lower=True).T


def gather_subcube(pieces, level_depth, leaf_index):
    for bit_number in range(level_depth):
        partner = swapped(pieces, "leaf", bit_number)
        upper_half = leaf_index >> bit_number & 1 == 1
        pieces = jnp.where(
            upper_half, jnp.concatenate([partner, pieces], 0), jnp.concatenate([pieces, partner], 0)
        )
    return pieces


def fetch_rows(pieces, wanted, level_depth, leaf_index):
    columns = pieces.shape[1]
    full_panel = gather_subcube(pieces, level_depth, leaf_index)
    return jnp.take(full_panel.reshape(FR // BLK, BLK, columns), wanted, axis=0).reshape(
        wanted.shape[0] * BLK, columns
    )


def merge_halves(placed, level_depth, leaf_index):
    for bit_number in reversed(range(level_depth)):
        middle = placed.shape[0] // 2
        upper_half = leaf_index >> bit_number & 1 == 1
        kept_half = jnp.where(upper_half, placed[middle:], placed[:middle])
        given_half = jnp.where(upper_half, placed[:middle], placed[middle:])
        placed = kept_half + swapped(given_half, "leaf", bit_number)
    return placed


def assemble(
    child_tile, initial, pattern, parent_map, level_depth, leaf_index, front_index, col_blocks
):
    group_share = 2**level_depth
    child_share = group_share // 2
    front_group = leaf_index // group_share
    child_side = leaf_index // child_share % 2
    child_sub = leaf_index % child_share
    sub_index = leaf_index % group_share
    update_blocks = UPD // BLK
    front_blocks = FR // BLK
    tile_cols = 2 * col_blocks * BLK
    gathered = lax.all_gather(child_tile, "front", axis=1, tiled=True)
    child_rows = gathered.shape[0]
    child_row_blocks = child_rows // BLK
    both_maps = lax.dynamic_index_in_dim(parent_map, front_group, 0, keepdims=False)
    block_map = lax.dynamic_index_in_dim(both_maps, child_side, 0, keepdims=False)[:update_blocks]
    target_cols = 2 * col_blocks * front_index + jnp.arange(2 * col_blocks, dtype=jnp.int32)
    col_pick = (block_map[:, None] == target_cols[None, :]).astype(jnp.float32)
    picked = jnp.einsum(
        "rik,it->rtk", gathered.reshape(child_rows, update_blocks, BLK), col_pick, precision=HIGHEST
    )
    my_map = lax.dynamic_slice_in_dim(block_map, child_sub * child_row_blocks, child_row_blocks)
    row_place = (jnp.arange(front_blocks, dtype=jnp.int32)[:, None] == my_map[None, :]).astype(
        jnp.float32
    )
    placed = jnp.einsum(
        "ba,akc->bkc",
        row_place,
        picked.reshape(child_row_blocks, BLK, tile_cols),
        precision=HIGHEST,
    ).reshape(FR, tile_cols)
    merged = merge_halves(placed, level_depth, leaf_index)
    own_blocks = front_blocks // group_share
    whole_pattern = lax.dynamic_index_in_dim(pattern, front_group, 0, keepdims=False)
    row_part = lax.dynamic_slice_in_dim(whole_pattern, sub_index * own_blocks, own_blocks, 0)
    row_part = lax.dynamic_slice_in_dim(row_part, 2 * col_blocks * front_index, 2 * col_blocks, 1)
    col_part = lax.dynamic_slice_in_dim(
        whole_pattern, 2 * col_blocks * front_index, 2 * col_blocks, 0
    )
    col_part = lax.dynamic_slice_in_dim(col_part, sub_index * own_blocks, own_blocks, 1)
    row_ids = sub_index * own_blocks + jnp.arange(own_blocks, dtype=jnp.int32)
    keep_blocks = (row_part == 1) | (col_part.T == 1) | (row_ids[:, None] == target_cols[None, :])
    keep_mask = (
        jnp.broadcast_to(keep_blocks[:, None, :, None], (own_blocks, BLK, 2 * col_blocks, BLK))
        .reshape(own_blocks * BLK, tile_cols)
        .astype(jnp.float32)
    )
    return (initial * keep_mask + merged, row_ids, target_cols)


def factor_panels(
    front_tile, row_ids, target_cols, level_depth, leaf_index, front_index, col_blocks
):
    tile_rows = front_tile.shape[0]
    panel_width = col_blocks * BLK
    row_odd = jnp.repeat(row_ids % 2 == 1, BLK)
    row_sep = jnp.repeat(row_ids // 2, BLK)
    col_odd = jnp.repeat(target_cols % 2 == 1, BLK)
    col_sep = jnp.repeat(target_cols // 2, BLK)
    factor_tile = jnp.zeros((tile_rows, col_blocks, BLK), jnp.float32)
    for step_index in range(lax.axis_size("front")):
        first_block = step_index * col_blocks
        panel_slots = first_block + jnp.arange(col_blocks, dtype=jnp.int32)
        sep_cols = front_tile.reshape(tile_rows, 2 * col_blocks, BLK)[:, 0::2].reshape(
            tile_rows, panel_width
        )
        panel_rows = spread(sep_cols, "front", step_index)
        wanted = jnp.concatenate([2 * panel_slots, target_cols])
        fetched = fetch_rows(panel_rows, wanted, level_depth, leaf_index)
        chol_block = jnp.linalg.cholesky(fetched[:panel_width])
        own_factor = solve_rows(chol_block, panel_rows)
        col_factor = solve_rows(chol_block, fetched[panel_width:])
        own_keep = (row_odd | (row_sep >= first_block + col_blocks)).astype(jnp.float32)
        col_keep = (col_odd | (col_sep >= first_block + col_blocks)).astype(jnp.float32)
        front_tile = front_tile - jnp.dot(
            own_factor * own_keep[:, None], (col_factor * col_keep[:, None]).T, precision=HIGHEST
        )
        valid_rows = (row_odd[:, None] | (row_sep[:, None] >= panel_slots[None, :])).astype(
            jnp.float32
        )
        factor_tile = jnp.where(
            front_index == step_index,
            own_factor.reshape(tile_rows, col_blocks, BLK) * valid_rows[:, :, None],
            factor_tile,
        )
    schur_tile = front_tile.reshape(tile_rows // BLK, BLK, 2 * col_blocks, BLK)[
        1::2, :, 1::2, :
    ].reshape(tile_rows // 2, col_blocks * BLK)
    return (factor_tile.reshape(tile_rows, col_blocks * BLK), schur_tile)


def per_device(
    child_updates,
    initial_one,
    initial_two,
    pattern_one,
    pattern_two,
    parent_map_one,
    parent_map_two,
):
    leaf_index = lax.axis_index("leaf")
    front_index = lax.axis_index("front")
    col_blocks = SEP // BLK // lax.axis_size("front")
    child_tile = child_updates
    factors = []
    for level_depth, initial, pattern, parent_map in (
        (1, initial_one, pattern_one, parent_map_one),
        (2, initial_two, pattern_two, parent_map_two),
    ):
        front_tile, row_ids, target_cols = assemble(
            child_tile,
            initial,
            pattern,
            parent_map,
            level_depth,
            leaf_index,
            front_index,
            col_blocks,
        )
        factor_tile, child_tile = factor_panels(
            front_tile, row_ids, target_cols, level_depth, leaf_index, front_index, col_blocks
        )
        factors.append(factor_tile)
    return (factors[0], factors[1], child_tile)


def solution(mesh):
    placed = (P("leaf", "front"), P("leaf", "front"), P("leaf", "front"), P(), P(), P(), P())
    return jax.shard_map(
        per_device,
        mesh=mesh,
        in_specs=placed,
        out_specs=(P("leaf", "front"), P("leaf", "front"), P("leaf", "front")),
        check_vma=False,
    )
```

profile of v0, /device:TPU:1, one launch (start us, length us, event | category | flops | bytes accessed | tf_op | source)
XLA Modules:
  0.0 1970.0 jit_solution(7487446941033398264)
XLA Ops:
  8.1 65.2 %all-gather.3.cloned.1.call-done = f32[1024,1024]{1,0:T(8,128)} async-done(((f32[1024,128]{1,0:T(8,128)}), f32[1024,1024]{1,0:T(8,128)}) %all-gather.3.cloned.1.call-update) | async-done | bytes 4194320 | tf_op jit(solution)/shard_map/all_gather | solution.py:74
  96.0 64.8 %all-reduce.17.cloned.1.call-done = f32[1024,128]{0,1:T(8,128)} async-done(((f32[1024,128]{0,1:T(8,128)}), f32[1024,128]{0,1:T(8,128)}) %all-reduce.17.cloned.1.call-update) | async-done | bytes 524304 | tf_op jit(solution)/shard_map/psum | solution.py:27
  172.7 11.7 cholesky.254
  185.8 9.8 custom-call.40
  198.7 67.0 %all-reduce.19.cloned.1.call-done = f32[1024,128]{0,1:T(8,128)} async-done(((f32[1024,128]{0,1:T(8,128)}), f32[1024,128]{0,1:T(8,128)}) %all-reduce.19.cloned.1.call-update) | async-done | bytes 524304 | tf_op jit(solution)/shard_map/psum | solution.py:27
  277.9 11.7 cholesky.265
  291.0 9.8 custom-call.42
  303.9 67.0 %all-reduce.21.cloned.1.call-done = f32[1024,128]{0,1:T(8,128)} async-done(((f32[1024,128]{0,1:T(8,128)}), f32[1024,128]{0,1:T(8,128)}) %all-reduce.21.cloned.1.call-update) | async-done | bytes 524304 | tf_op jit(solution)/shard_map/psum | solution.py:27
  382.9 11.7 cholesky.276
  395.9 9.8 custom-call.44
  408.9 67.0 %all-reduce.23.cloned.1.call-done = f32[1024,128]{0,1:T(8,128)} async-done(((f32[1024,128]{0,1:T(8,128)}), f32[1024,128]{0,1:T(8,128)}) %all-reduce.23.cloned.1.call-update) | async-done | bytes 524304 | tf_op jit(solution)/shard_map/psum | solution.py:27
  488.0 11.7 cholesky.287
  501.1 9.8 custom-call.46
  513.9 67.0 %all-reduce.25.cloned.1.call-done = f32[1024,128]{0,1:T(8,128)} async-done(((f32[1024,128]{0,1:T(8,128)}), f32[1024,128]{0,1:T(8,128)}) %all-reduce.25.cloned.1.call-update) | async-done | bytes 524304 | tf_op jit(solution)/shard_map/psum | solution.py:27
  593.1 11.7 cholesky.298
  619.1 67.0 %all-reduce.27.cloned.1.call-done = f32[1024,128]{0,1:T(8,128)} async-done(((f32[1024,128]{0,1:T(8,128)}), f32[1024,128]{0,1:T(8,128)}) %all-reduce.27.cloned.1.call-update) | async-done | bytes 524304 | tf_op jit(solution)/shard_map/psum | solution.py:27
  698.4 11.7 cholesky.309
  724.3 67.1 %all-reduce.29.cloned.1.call-done = f32[1024,128]{0,1:T(8,128)} async-done(((f32[1024,128]{0,1:T(8,128)}), f32[1024,128]{0,1:T(8,128)}) %all-reduce.29.cloned.1.call-update) | async-done | bytes 524304 | tf_op jit(solution)/shard_map/psum | solution.py:27
  803.4 11.7 cholesky.320
  829.3 67.1 %all-reduce.31.cloned.1.call-done = f32[1024,128]{0,1:T(8,128)} async-done(((f32[1024,128]{0,1:T(8,128)}), f32[1024,128]{0,1:T(8,128)}) %all-reduce.31.cloned.1.call-update) | async-done | bytes 524304 | tf_op jit(solution)/shard_map/psum | solution.py:27
  908.4 11.7 cholesky.331
  936.3 40.7 %all-gather.5.cloned.1.call-done = f32[512,1024]{1,0:T(8,128)} async-done(((f32[512,128]{1,0:T(8,128)}), f32[512,1024]{1,0:T(8,128)}) %all-gather.5.cloned.1.call-update) | async-done | bytes 2097168 | tf_op jit(solution)/shard_map/all_gather | solution.py:74
  987.9 15.9 collective-permute-done.9
  1016.5 65.7 %all-reduce.33.cloned.1.call-done = f32[512,128]{0,1:T(8,128)} async-done(((f32[512,128]{0,1:T(8,128)}), f32[512,128]{0,1:T(8,128)}) %all-reduce.33.cloned.1.call-update) | async-done | bytes 262160 | tf_op jit(solution)/shard_map/psum | solution.py:27
  1091.7 11.8 collective-permute-done.12
  1107.2 11.7 cholesky.342
  1132.3 67.0 %all-reduce.35.cloned.1.call-done = f32[512,128]{0,1:T(8,128)} async-done(((f32[512,128]{0,1:T(8,128)}), f32[512,128]{0,1:T(8,128)}) %all-reduce.35.cloned.1.call-update) | async-done | bytes 262160 | tf_op jit(solution)/shard_map/psum | solution.py:27
  1208.6 11.8 collective-permute-done.14
  1224.1 11.7 cholesky.353
  1249.3 67.1 %all-reduce.37.cloned.1.call-done = f32[512,128]{0,1:T(8,128)} async-done(((f32[512,128]{0,1:T(8,128)}), f32[512,128]{0,1:T(8,128)}) %all-reduce.37.cloned.1.call-update) | async-done | bytes 262160 | tf_op jit(solution)/shard_map/psum | solution.py:27
  1325.7 11.8 collective-permute-done.16
  1341.2 11.7 cholesky.364
  1366.4 67.0 %all-reduce.39.cloned.1.call-done = f32[512,128]{0,1:T(8,128)} async-done(((f32[512,128]{0,1:T(8,128)}), f32[512,128]{0,1:T(8,128)}) %all-reduce.39.cloned.1.call-update) | async-done | bytes 262160 | tf_op jit(solution)/shard_map/psum | solution.py:27
  1442.7 11.8 collective-permute-done.18
  1458.2 11.7 cholesky.375
  1483.5 67.0 %all-reduce.41.cloned.1.call-done = f32[512,128]{0,1:T(8,128)} async-done(((f32[512,128]{0,1:T(8,128)}), f32[512,128]{0,1:T(8,128)}) %all-reduce.41.cloned.1.call-update) | async-done | bytes 262160 | tf_op jit(solution)/shard_map/psum | solution.py:27
  1560.0 11.8 collective-permute-done.20
  1575.5 11.7 cholesky.386
  1600.8 67.0 %all-reduce.43.cloned.1.call-done = f32[512,128]{0,1:T(8,128)} async-done(((f32[512,128]{0,1:T(8,128)}), f32[512,128]{0,1:T(8,128)}) %all-reduce.43.cloned.1.call-update) | async-done | bytes 262160 | tf_op jit(solution)/shard_map/psum | solution.py:27
  1677.0 11.8 collective-permute-done.22
  1692.5 11.7 cholesky.397
  1705.6 9.8 custom-call.66
  1718.5 67.0 %all-reduce.45.cloned.1.call-done = f32[512,128]{0,1:T(8,128)} async-done(((f32[512,128]{0,1:T(8,128)}), f32[512,128]{0,1:T(8,128)}) %all-reduce.45.cloned.1.call-update) | async-done | bytes 262160 | tf_op jit(solution)/shard_map/psum | solution.py:27
  1795.9 10.7 collective-permute-done.24
  1810.3 11.7 cholesky.408
  1823.4 10.4 custom-call.68
  1840.7 67.0 %all-reduce.47.cloned.1.call-done = f32[512,128]{0,1:T(8,128)} async-done(((f32[512,128]{0,1:T(8,128)}), f32[512,128]{0,1:T(8,128)}) %all-reduce.47.cloned.1.call-update) | async-done | bytes 262160 | tf_op jit(solution)/shard_map/psum | solution.py:27
  1935.3 11.7 cholesky.419
  (617 shorter events, 433.0 us)
Async XLA Ops:
  7.2 66.1 %all-gather.3.cloned.1.call-start = ((), (), s32[]{:S(2)}) async-start(), calls=%async_computation | async-start | bytes 4718592 | tf_op jit(solution)/shard_map/all_gather | solution.py:74
  7.9 152.8 %all-reduce.17.cloned.1.call-start = ((), (), s32[]{:S(2)}) async-start(), calls=%async_computation.1 | async-start | bytes 1048576 | tf_op jit(solution)/shard_map/psum | solution.py:27
  82.8 10.4 collective-permute-start
  95.8 169.9 %all-reduce.19.cloned.1.call-start = ((), (), s32[]{:S(2)}) async-start(), calls=%async_computation.2 | async-start | bytes 1048576 | tf_op jit(solution)/shard_map/psum | solution.py:27
  95.9 812.2 %copy-start.63 = (pred[3]{0:T(512)(128)(4,1)}, pred[3]{0:T(512)(128)(4,1)S(1)}, u32[]{:S(2)}) copy-start(pred[3]{0:T(512)(128)(4,1)S(1)} %get-tuple-element.14) | copy-start | bytes 13
  160.7 7.2 collective-permute-start.1
  198.6 172.3 %all-reduce.21.cloned.1.call-start = ((), (), s32[]{:S(2)}) async-start(), calls=%async_computation.3 | async-start | bytes 1048576 | tf_op jit(solution)/shard_map/psum | solution.py:27
  265.7 7.4 collective-permute-start.2
  303.8 172.1 %all-reduce.23.cloned.1.call-start = ((), (), s32[]{:S(2)}) async-start(), calls=%async_computation.4 | async-start | bytes 1048576 | tf_op jit(solution)/shard_map/psum | solution.py:27
  303.9 602.3 %copy-start.62 = (s32[1024]{0:T(1024)}, s32[1024]{0:T(1024)S(1)}, u32[]{:S(2)}) copy-start(s32[1024]{0:T(1024)S(1)} %get-tuple-element.48) | copy-start | bytes 12292
  370.9 7.1 collective-permute-start.3
  408.7 172.2 %all-reduce.25.cloned.1.call-start = ((), (), s32[]{:S(2)}) async-start(), calls=%async_computation.5 | async-start | bytes 1048576 | tf_op jit(solution)/shard_map/psum | solution.py:27
  475.9 7.2 collective-permute-start.4
  513.9 172.2 %all-reduce.27.cloned.1.call-start = ((), (), s32[]{:S(2)}) async-start(), calls=%async_computation.6 | async-start | bytes 1048576 | tf_op jit(solution)/shard_map/psum | solution.py:27
  581.0 7.2 collective-permute-start.5
  619.0 172.4 %all-reduce.29.cloned.1.call-start = ((), (), s32[]{:S(2)}) async-start(), calls=%async_computation.7 | async-start | bytes 1048576 | tf_op jit(solution)/shard_map/psum | solution.py:27
  686.1 7.4 collective-permute-start.6
  724.2 172.1 %all-reduce.31.cloned.1.call-start = ((), (), s32[]{:S(2)}) async-start(), calls=%async_computation.8 | async-start | bytes 1048576 | tf_op jit(solution)/shard_map/psum | solution.py:27
  791.4 7.1 collective-permute-start.7
  829.2 147.8 %all-gather.5.cloned.1.call-start = ((), (), s32[]{:S(2)}) async-start(), calls=%async_computation.9 | async-start | bytes 2359296 | tf_op jit(solution)/shard_map/all_gather | solution.py:74
  896.4 7.2 collective-permute-start.8
  935.2 147.0 %all-reduce.33.cloned.1.call-start = ((), (), s32[]{:S(2)}) async-start(), calls=%async_computation.10 | async-start | bytes 524288 | tf_op jit(solution)/shard_map/psum | solution.py:27
  983.8 20.0 %collective-permute-start.9 = (f32[1024,256]{0,1:T(8,128)}, f32[1024,256]{0,1:T(8,128)}, u32[]{:S(2)}, u32[]{:S(2)}) collective-permute-start(f32[1024,256]{0,1:T(8,128)} %copy.86), channel_id=1, source_target_pairs={{0,16},{16,0},{8,24},{24,8},{32,48},{48,32},{40,56},{56,40},{64,80... | collective-permute-start | bytes 3145736 | tf_op jit(solution)/shard_map/ppermute | solution.py:22
  1005.3 9.0 collective-permute-start.10
  1016.5 182.9 %all-reduce.35.cloned.1.call-start = ((), (), s32[]{:S(2)}) async-start(), calls=%async_computation.11 | async-start | bytes 524288 | tf_op jit(solution)/shard_map/psum | solution.py:27
  1082.2 6.6 collective-permute-start.11
  1089.8 13.7 collective-permute-start.12
  1132.3 184.1 %all-reduce.37.cloned.1.call-start = ((), (), s32[]{:S(2)}) async-start(), calls=%async_computation.12 | async-start | bytes 524288 | tf_op jit(solution)/shard_map/psum | solution.py:27
  1199.4 6.6 collective-permute-start.13
  1207.0 13.4 collective-permute-start.14
  1249.3 184.1 %all-reduce.39.cloned.1.call-start = ((), (), s32[]{:S(2)}) async-start(), calls=%async_computation.13 | async-start | bytes 524288 | tf_op jit(solution)/shard_map/psum | solution.py:27
  1316.4 6.6 collective-permute-start.15
  1324.1 13.4 collective-permute-start.16
  1366.4 184.1 %all-reduce.41.cloned.1.call-start = ((), (), s32[]{:S(2)}) async-start(), calls=%async_computation.14 | async-start | bytes 524288 | tf_op jit(solution)/shard_map/psum | solution.py:27
  1433.4 6.6 collective-permute-start.17
  1441.1 13.5 collective-permute-start.18
  1483.4 184.4 %all-reduce.43.cloned.1.call-start = ((), (), s32[]{:S(2)}) async-start(), calls=%async_computation.15 | async-start | bytes 524288 | tf_op jit(solution)/shard_map/psum | solution.py:27
  1550.5 6.6 collective-permute-start.19
  1558.2 13.7 collective-permute-start.20
  1600.7 184.8 %all-reduce.45.cloned.1.call-start = ((), (), s32[]{:S(2)}) async-start(), calls=%async_computation.16 | async-start | bytes 524288 | tf_op jit(solution)/shard_map/psum | solution.py:27
  1667.8 6.6 collective-permute-start.21
  1675.5 13.4 collective-permute-start.22
  1716.2 90.6 %copy-start.23 = (f32[128,512]{1,0:T(8,128)}, f32[128,512]{1,0:T(8,128)S(1)}, u32[]{:S(2)}) copy-start(f32[128,512]{1,0:T(8,128)S(1)} %fusion.49) | copy-start | bytes 786436
  1718.4 189.3 %all-reduce.47.cloned.1.call-start = ((), (), s32[]{:S(2)}) async-start(), calls=%async_computation.17 | async-start | bytes 524288 | tf_op jit(solution)/shard_map/psum | solution.py:27
  1785.5 6.6 collective-permute-start.23
  1793.2 13.4 collective-permute-start.24
  1907.7 6.6 collective-permute-start.25
  1916.1 13.7 collective-permute-start.26
  (65 other events, 1790.7 us)
Sparse Core Ops, SparseCore 0:
  9.7 63.4 all-gather.2
  95.9 64.7 all-reduce.16
  198.7 66.9 all-reduce.18
  303.9 66.9 all-reduce.20
  408.9 67.0 all-reduce.22
  514.0 66.9 all-reduce.24
  619.1 66.9 all-reduce.26
  724.3 66.9 all-reduce.28
  829.3 66.9 all-reduce.30
  935.3 41.6 all-gather.4
  1016.6 65.5 all-reduce.32
  1132.4 66.9 all-reduce.34
  1249.4 66.9 all-reduce.36
  1366.5 66.9 all-reduce.38
  1483.5 66.9 all-reduce.40
  1600.8 66.9 all-reduce.42
  1718.6 66.9 all-reduce.44
  1840.7 66.9 all-reduce.46
where the time goes:
time: 1980 us; the launch traced here: 1970 us
  waiting for transfers between devices  1300 us (66%)
  other arithmetic  415 us (21%)
  starting transfers between devices  111 us (6%)
  local copies, waits for them, and re-layouts  86 us (4%)
  matrix products  35.7 us (2%)
    psum x16, waiting for transfers between devices, spread(): return lax.psum(block, axis)  1070 us
    another operation x48, other arithmetic, factor_panels(): chol_block = jnp.linalg.cholesky(fetched[:panel_width])  198 us
    another operation x32, other arithmetic, solve_rows(): jax.scipy.linalg.solve_triangular(chol_block, right_side.T, lower=True)  168 us
    ppermute x27, waiting for transfers between devices, swapped(): return lax.ppermute(block, axis, route)  128 us
    ppermute x27, starting transfers between devices, swapped(): return lax.ppermute(block, axis, route)  110 us
    all_gather x2, waiting for transfers between devices, assemble(): gathered = lax.all_gather(child_tile, 'front', axis=1, tiled=True)  106 us
  transfers between devices with their start and end apart: 45, of which 43 were waited for; matrix products, arithmetic and copies ran while one was open for 1% of the time, Pallas kernels for 0%

commit v1 on v0

v1 whole, which is shorter than its diff:
```python
import jax
import jax.numpy as jnp
from jax import lax
from jax.experimental import pallas as pl
from jax.experimental.pallas import tpu as pltpu
from jax.sharding import Mesh, PartitionSpec as P

BLK = 128
NB = 8
FB = 16
F32 = jnp.float32
BF16 = jnp.bfloat16
VMEM = pl.BlockSpec(memory_space=pltpu.VMEM)
SMEM = pl.BlockSpec(memory_space=pltpu.SMEM)
PARAMS = pltpu.CompilerParams(vmem_limit_bytes=58 * 1024 * 1024)
LEAF = ("x", "yh", "yl", "core")


def shape(*dims):
    return jax.ShapeDtypeStruct(dims, F32)


def packed_index(row, col):
    return col * NB - col * (col - 1) // 2 + row - col


def across(piece):
    return jnp.broadcast_to(piece, (8, BLK))


def factor_block(block):
    sub = lax.broadcasted_iota(jnp.int32, (8, BLK), 0)
    lane = lax.broadcasted_iota(jnp.int32, (8, BLK), 1)
    rows = [block[8 * g : 8 * g + 8] for g in range(16)]
    diag = jnp.zeros((8, BLK), F32)
    for t in range(16):
        cols = {}
        for b in range(8):
            for g in range(t, 16):
                cols[b, g] = across(rows[g][:, 8 * t + b : 8 * t + b + 1])
        for b in range(8):
            here = lane == 8 * t + b
            pivot = across(cols[b, t][b : b + 1])
            scale = lax.rsqrt(pivot)
            diag = jnp.where(here, pivot * scale, diag)
            low = {g: cols[b, g] * scale for g in range(t, 16)}
            for later in range(b + 1, 8):
                weight = across(low[t][later : later + 1])
                for g in range(t, 16):
                    cols[later, g] = cols[later, g] - low[g] * weight
            row = jnp.where(here, scale, across(rows[t][b : b + 1]) * scale)
            lower = jnp.where(here, 0.0, rows[t]) - low[t] * row
            rows[t] = jnp.where(sub == b, row, jnp.where(sub > b, lower, rows[t]))
            for g in range(t + 1, 16):
                rows[g] = jnp.where(here, 0.0, rows[g]) - low[g] * row
    full = jnp.concatenate(rows, 0)
    row_id = lax.broadcasted_iota(jnp.int32, (BLK, BLK), 0)
    col_id = lax.broadcasted_iota(jnp.int32, (BLK, BLK), 1)
    on_diag = jnp.broadcast_to(diag[0:1], (BLK, BLK))
    upper = jnp.where(col_id > row_id, full, jnp.where(col_id == row_id, on_diag, 0.0))
    return upper.T, jnp.where(col_id <= row_id, full, 0.0)


def halves(value):
    high = value.astype(BF16)
    return high, (value - high.astype(F32)).astype(BF16)


def dot_nt(left, right):
    return lax.dot_general(
        left, right, (((1,), (1,)), ((), ())), preferred_element_type=F32
    )


def dot_split(left, right):
    left_high, left_low = halves(left)
    right_high, right_low = halves(right)
    return dot_nt(
        jnp.concatenate([left_high, left_high, left_low], 1),
        jnp.concatenate([right_high, right_low, right_high], 1),
    )


def factor_corner(work, chol, inverse):
    order = NB * BLK

    def one_panel(step, carry):
        first = pl.multiple_of(step * BLK, BLK)
        lower, lower_inverse = factor_block(work[step, pl.ds(first, BLK), :])
        chol[step, pl.ds(first, BLK), :] = lower
        inverse[step] = lower_inverse
        for j in range(NB - 1):

            @pl.when(step == j)
            def _():
                start = BLK * (j + 1)
                panel = dot_split(work[j, start:, :], inverse[j])
                chol[j, start:, :] = panel
                high, low = halves(panel)
                left = jnp.concatenate([high, high, low], 1)
                right = jnp.concatenate([high, low, high], 1)
                for k in range(j + 1, NB, 2):
                    wide = min(2, NB - k)
                    top = BLK * k - start
                    update = dot_nt(left[top:], right[top : top + wide * BLK])
                    for w in range(wide):
                        work[k + w, BLK * k :, :] = (
                            work[k + w, BLK * k :, :] - update[:, w * BLK : (w + 1) * BLK]
                        )

        return carry

    for j in range(1, NB):
        chol[j, : j * BLK, :] = jnp.zeros((j * BLK, BLK), F32)
    lax.fori_loop(0, NB, one_panel, 0)


def solve_rows(right_side, chol, inverse, solved, solved_high, solved_low):
    for p in range(0, NB, 2):
        first, second = right_side(p), right_side(p + 1)
        if p:
            depth = range(p)
            left_high = jnp.concatenate([solved_high[k] for k in depth], 1)
            left_low = jnp.concatenate([solved_low[k] for k in depth], 1)
            right = jnp.concatenate([chol[k, p * BLK : (p + 2) * BLK, :] for k in depth], 1)
            right_high, right_low = halves(right)
            update = (
                dot_nt(left_high, right_high)
                + dot_nt(left_high, right_low)
                + dot_nt(left_low, right_high)
            )
            first = first - update[:, :BLK]
            second = second - update[:, BLK:]
        first = dot_split(first, inverse[p])
        second = second - dot_split(first, chol[p, (p + 1) * BLK : (p + 2) * BLK, :])
        second = dot_split(second, inverse[p + 1])
        for k, value in ((p, first), (p + 1, second)):
            solved[k] = value
            solved_high[k], solved_low[k] = halves(value)


def place_of(block_map, front, child, slots):
    for m in range(FB):
        slots[child, m] = -1
    for i in range(NB):
        slots[child, block_map[front, child, i]] = i


def kept(pattern, front, row, col):
    return (pattern[front, row, col] == 1) | (pattern[front, col, row] == 1) | (row == col)


def pack_kernel(ids, map_one, pattern_two, child, initial_two, packed, sep_two, row_two, tail_two):
    front_one, side, z, front_two, sub = ids[0], ids[1], ids[2], ids[3], ids[4]
    packed[...] = jnp.zeros_like(packed)
    for i in range(NB):
        packed[map_one[front_one, side, i]] = child[i * BLK : (i + 1) * BLK, :].T
    for r in range(4):
        for w in range(2):
            keep = kept(pattern_two, front_two, 4 * sub + r, 2 * z + w)
            tile = initial_two[r * BLK : (r + 1) * BLK, w * BLK : (w + 1) * BLK]
            tile = jnp.where(keep, tile, 0.0)
            if w == 0:
                sep_two[r % 2 * 2 + r // 2] = tile
            elif r % 2 == 0:
                row_two[r // 2] = tile.T
            else:
                tail_two[r // 2] = tile


def assemble_kernel(
    ids, map_one, pattern_one, own, other, initial, corner, lower, trailing, slots
):
    front_one, side, z = ids[0], ids[1], ids[2]
    place_of(map_one, front_one, 0, slots)
    place_of(map_one, front_one, 1, slots)
    for r in range(NB):
        row = NB * side + r
        for w in range(2):
            if r % 2 == 0 and w == 1:
                continue
            out = (lower if w == 0 else trailing) if r % 2 else corner
            keep = kept(pattern_one, front_one, row, 2 * z + w)
            tile = initial[r * BLK : (r + 1) * BLK, w * BLK : (w + 1) * BLK]
            out[r // 2] = jnp.where(keep, tile, 0.0)
            for source, child in ((own, side), (other, 1 - side)):
                index = slots[child, row]

                @pl.when(index >= 0)
                def _():
                    out[r // 2] = out[r // 2] + source[index, w]


def chol_kernel(ids, own, other, chol, inverse, work):
    side = ids[1]
    half = NB // 2 * BLK
    work[:, pl.ds(pl.multiple_of(side * half, half), half), :] = own[...]
    work[:, pl.ds(pl.multiple_of((1 - side) * half, half), half), :] = other[...]
    factor_corner(work, chol, inverse)


def rest_kernel(
    ids,
    chol,
    inverse,
    lower_own,
    lower_other,
    trail_own,
    trail_other,
    factor,
    packed,
    lower,
    solved,
    solved_high,
    solved_low,
    trail,
):
    side, z = ids[1], ids[2]
    half = NB // 2 * BLK
    for ref, own, other in ((lower, lower_own, lower_other), (trail, trail_own, trail_other)):
        ref[:, pl.ds(pl.multiple_of(side * half, half), half), :] = own[...]
        ref[:, pl.ds(pl.multiple_of((1 - side) * half, half), half), :] = other[...]
    solve_rows(lambda k: lower[k], chol, inverse, solved, solved_high, solved_low)
    for p in range(0, NB, 2):
        high = jnp.concatenate([solved_high[k, p * BLK :, :] for k in range(NB)], 1)
        low = jnp.concatenate([solved_low[k, p * BLK :, :] for k in range(NB)], 1)
        wide_high, wide_low = high[: 2 * BLK], low[: 2 * BLK]
        update = dot_nt(high, wide_high) + dot_nt(high, wide_low) + dot_nt(low, wide_high)
        for w in range(2):
            for i in range(p + w, NB):
                packed[packed_index(i, p + w)] = (
                    trail[p + w, i * BLK : (i + 1) * BLK, :]
                    - update[(i - p) * BLK : (i - p + 1) * BLK, w * BLK : (w + 1) * BLK]
                )
    for r in range(NB):
        source = solved if r % 2 else chol
        start = pl.multiple_of((side * (NB // 2) + r // 2) * BLK, BLK)
        factor[r * BLK : (r + 1) * BLK, :] = source[z, pl.ds(start, BLK), :]


def second_kernel(
    ids,
    map_two,
    corner_own,
    corner_yl,
    corner_core,
    corner_both,
    lower_own,
    row_own,
    row_yl,
    row_core,
    row_both,
    tail,
    child_half_own,
    child_half_other,
    child_far_own,
    child_far_other,
    factor,
    schur,
    work,
    chol,
    inverse,
    lower,
    solved,
    solved_high,
    solved_low,
    trail,
    slots,
):
    side, z, front, sub = ids[1], ids[2], ids[3], ids[4]
    mine = sub // 2
    for ref, yl, core in (
        (corner_own, mine, side),
        (corner_yl, 1 - mine, side),
        (corner_core, mine, 1 - side),
        (corner_both, 1 - mine, 1 - side),
    ):
        start = pl.multiple_of((yl * 2 + core) * 2 * BLK, 2 * BLK)
        work[:, pl.ds(start, 2 * BLK), :] = ref[...]
    lower[:, : 2 * BLK, :] = lower_own[...]
    for ref, yl, core in (
        (row_own, mine, side),
        (row_yl, 1 - mine, side),
        (row_core, mine, 1 - side),
        (row_both, 1 - mine, 1 - side),
    ):
        at = (yl * 2 + core) * 2
        for b in range(2):
            lower[at + b, 2 * BLK :, :] = ref[b]
    for r in range(2):
        trail[r] = tail[r]
    place_of(map_two, front, 0, slots)
    place_of(map_two, front, 1, slots)
    wanted = (2 * sub, 2 * sub + 1, z)

    for child in range(2):
        near = mine == child

        for i in range(NB):
            for k in range(i + 1):
                index = packed_index(i, k)
                half_id, at = divmod(index, 18)
                row, col = map_two[front, child, i], map_two[front, child, k]
                row_half, col_half = row // 2, col // 2
                row_odd, col_odd = row % 2, col % 2

                def block():
                    from_near = jnp.where(
                        side == half_id, child_half_own[at], child_half_other[at]
                    )
                    from_far = jnp.where(side == half_id, child_far_own[at], child_far_other[at])
                    return jnp.where(near, from_near, from_far)

                @pl.when((row_odd == 0) & (col_odd == 0) & (row_half >= col_half))
                def _():
                    start = pl.multiple_of(row_half * BLK, BLK)
                    work[col_half, pl.ds(start, BLK), :] += block()

                @pl.when((row_odd == 0) & (col_odd == 0) & (row_half < col_half))
                def _():
                    start = pl.multiple_of(col_half * BLK, BLK)
                    work[row_half, pl.ds(start, BLK), :] += block().T

                @pl.when((row_odd == 1) & (col_odd == 0))
                def _():
                    for slot, target in enumerate(wanted):

                        @pl.when(row_half == target)
                        def _():
                            lower[col_half, slot * BLK : (slot + 1) * BLK, :] += block()

                @pl.when((row_odd == 0) & (col_odd == 1))
                def _():
                    for slot, target in enumerate(wanted):

                        @pl.when(col_half == target)
                        def _():
                            lower[row_half, slot * BLK : (slot + 1) * BLK, :] += block().T

                @pl.when((row_odd == 1) & (col_odd == 1))
                def _():
                    for slot in range(2):

                        @pl.when((row_half == wanted[slot]) & (col_half == z))
                        def _():
                            trail[slot] += block()

                        if i != k:

                            @pl.when((col_half == wanted[slot]) & (row_half == z))
                            def _():
                                trail[slot] += block().T

    factor_corner(work, chol, inverse)
    solve_rows(lambda k: lower[k], chol, inverse, solved, solved_high, solved_low)
    high = jnp.concatenate([solved_high[k] for k in range(NB)], 1)
    low = jnp.concatenate([solved_low[k] for k in range(NB)], 1)
    left_high, left_low = high[: 2 * BLK], low[: 2 * BLK]
    right_high, right_low = high[2 * BLK :], low[2 * BLK :]
    update = (
        dot_nt(left_high, right_high)
        + dot_nt(left_high, right_low)
        + dot_nt(left_low, right_high)
    )
    for r in range(2):
        schur[r * BLK : (r + 1) * BLK, :] = trail[r] - update[r * BLK : (r + 1) * BLK, :]
        start = pl.multiple_of((2 * sub + r) * BLK, BLK)
        factor[2 * r * BLK : (2 * r + 1) * BLK, :] = chol[z, pl.ds(start, BLK), :]
        factor[(2 * r + 1) * BLK : (2 * r + 2) * BLK, :] = solved[z, r * BLK : (r + 1) * BLK, :]


def call(kernel, name, outs, specs, args, scratch=()):
    return pl.pallas_call(
        kernel,
        name=name,
        out_shape=outs,
        in_specs=specs,
        out_specs=[VMEM] * len(outs),
        scratch_shapes=list(scratch),
        compiler_params=PARAMS,
    )(*args)


def swap(value, axis):
    return lax.ppermute(value, axis, [(0, 1), (1, 0)])


def per_device(
    child_updates,
    initial_one,
    initial_two,
    pattern_one,
    pattern_two,
    parent_map_one,
    parent_map_two,
):
    x, yh, yl = lax.axis_index("x"), lax.axis_index("yh"), lax.axis_index("yl")
    core, z = lax.axis_index("core"), lax.axis_index("front")
    ids = jnp.stack([x * 4 + yh * 2 + yl, core, z, x * 2 + yh, yl * 2 + core]).astype(jnp.int32)
    panel = (NB, NB * BLK, BLK)

    packed, sep_two, row_two, tail_two = call(
        pack_kernel,
        "pack",
        [shape(FB, BLK, BLK), shape(4, BLK, BLK), shape(2, BLK, BLK), shape(2, BLK, BLK)],
        [SMEM, SMEM, SMEM, VMEM, VMEM],
        (ids, parent_map_one, pattern_two, child_updates, initial_two),
    )
    own = lax.all_to_all(packed.reshape(NB, 2, BLK, BLK), "front", 0, 0, tiled=True)
    other = swap(own, "core")
    corner, lower, trailing = call(
        assemble_kernel,
        "assemble",
        [shape(4, BLK, BLK)] * 3,
        [SMEM, SMEM, SMEM, VMEM, VMEM, VMEM],
        (ids, parent_map_one, pattern_one, own, other, initial_one),
        [pltpu.SMEM((2, FB), jnp.int32)],
    )

    def spread(value):
        flat = value.reshape(-1, BLK)
        return lax.all_gather(flat, "front", axis=0, tiled=False)

    corner_all = spread(corner)
    chol, inverse = call(
        chol_kernel,
        "chol",
        [shape(*panel), shape(NB, BLK, BLK)],
        [SMEM, VMEM, VMEM],
        (ids, corner_all, swap(corner_all, "core")),
        [pltpu.VMEM(panel, F32)],
    )
    lower_all = spread(lower)
    trail_all = spread(trailing)
    factor_one, schur_one = call(
        rest_kernel,
        "rest",
        [shape(NB * BLK, BLK), shape(36, BLK, BLK)],
        [SMEM] + [VMEM] * 6,
        (
            ids,
            chol,
            inverse,
            lower_all,
            swap(lower_all, "core"),
            trail_all,
            swap(trail_all, "core"),
        ),
        [pltpu.VMEM(panel, F32)] * 2
        + [pltpu.VMEM(panel, BF16)] * 2
        + [pltpu.VMEM(panel, F32)],
    )

    gathered_two = spread(sep_two)
    corner_near = gathered_two[:, : 2 * BLK]
    lower_near = gathered_two[:, 2 * BLK :]
    corner_yl = swap(corner_near, "yl")
    row_yl = swap(row_two, "yl")

    half_near = jnp.where(core == 0, schur_one[:18], schur_one[18:])
    half_far = swap(half_near, "yl")
    far_other = swap(half_far, "core")
    near_other = jnp.where(core == 0, schur_one[18:], schur_one[:18])
    factor_two, schur_two = call(
        second_kernel,
        "second",
        [shape(4 * BLK, BLK), shape(2 * BLK, BLK)],
        [SMEM, SMEM] + [VMEM] * 14,
        (
            ids,
            parent_map_two,
            corner_near,
            corner_yl,
            swap(corner_near, "core"),
            swap(corner_yl, "core"),
            lower_near,
            row_two,
            row_yl,
            swap(row_two, "core"),
            swap(row_yl, "core"),
            tail_two,
            half_near,
            near_other,
            half_far,
            far_other,
        ),
        [
            pltpu.VMEM(panel, F32),
            pltpu.VMEM(panel, F32),
            pltpu.VMEM((NB, BLK, BLK), F32),
            pltpu.VMEM((NB, 3 * BLK, BLK), F32),
            pltpu.VMEM((NB, 3 * BLK, BLK), F32),
            pltpu.VMEM((NB, 3 * BLK, BLK), BF16),
            pltpu.VMEM((NB, 3 * BLK, BLK), BF16),
            pltpu.VMEM((2, BLK, BLK), F32),
            pltpu.SMEM((2, FB), jnp.int32),
        ],
    )
    return factor_one, factor_two, schur_two


def solution(mesh):
    cut = Mesh(mesh.devices.reshape(4, 2, 2, 2, 8), LEAF + ("front",))
    tile = P(LEAF, "front")
    return jax.shard_map(
        per_device,
        mesh=cut,
        in_specs=(tile, tile, tile, P(), P(), P(), P()),
        out_specs=(tile, tile, tile),
        check_vma=False,
    )
```

time: 1980 us -> 382 us (0.19)
  waiting for transfers between devices: 1300 us -> 159 us
  other arithmetic: 415 us -> 2.89 us
  Pallas kernels: 0 us -> 133 us
  starting transfers between devices: 111 us -> 22.3 us
  local copies, waits for them, and re-layouts: 86 us -> 7.58 us
  blocking collectives: 0 us -> 36.2 us
  matrix products: 35.7 us -> 0 us
    psum x16 -> x0, waiting for transfers between devices: 1070 us -> none  [spread(): return lax.psum(block, axis)]
    another operation x80 -> x0, other arithmetic: 366 us -> none  [the longest x48 198 us: factor_panels(): chol_block = jnp.linalg.cholesky(fetched[:panel_width])]
    pallas_call x0 -> x5, Pallas kernels: none -> 133 us  [call(): pl.pallas_call(kernel, name=name, out_shape=outs, in_specs=specs, out_spe...]
    ppermute x27 -> x12, starting transfers between devices: 110 us -> 22.1 us  [swap(): return lax.ppermute(value, axis, [(0, 1), (1, 0)])]
    ppermute x27 -> x12, waiting for transfers between devices: 128 us -> 51.2 us  [swap(): return lax.ppermute(value, axis, [(0, 1), (1, 0)])]
    select_n x61 -> x1, other arithmetic: 40.3 us -> 2.89 us  [per_device(): near_other = jnp.where(core == 0, schur_one[18:], schur_one[:18])]
    all_to_all x0 -> x1, blocking collectives: none -> 36.2 us  [per_device(): lax.all_to_all(packed.reshape(NB, 2, BLK, BLK), 'front', 0, 0, tiled=True)]
    gather x32 -> x0, local copies, waits for them, and re-layouts: 31 us -> none  [fetch_rows(): jnp.take(full_panel.reshape(FR // BLK, BLK, columns), wanted, axis=0)]
  transfers between devices with their start and end apart: 45 -> 16, of which waited for: 43 -> 8; matrix products, arithmetic and copies ran while one was open for 1% -> 2% of each run, Pallas kernels for 0% -> 17%
where the time goes in v1:
time: 382 us; the launch traced here: 375 us
  waiting for transfers between devices  159 us (42%)
  Pallas kernels  133 us (35%)
  blocking collectives  36.2 us (9%)
  starting transfers between devices  22.3 us (6%)
  between operations  14.3 us (4%)
  local copies, waits for them, and re-layouts  7.58 us (2%)
    pallas_call x5, Pallas kernels, call(): pl.pallas_call(kernel, name=name, out_shape=outs, in_specs=specs, out_spe...  133 us
    all_gather x4, waiting for transfers between devices, spread(): return lax.all_gather(flat, 'front', axis=0, tiled=False)  106 us
    ppermute x12, waiting for transfers between devices, swap(): return lax.ppermute(value, axis, [(0, 1), (1, 0)])  51.2 us
    all_to_all x1, blocking collectives, per_device(): lax.all_to_all(packed.reshape(NB, 2, BLK, BLK), 'front', 0, 0, tiled=True)  36.2 us
    ppermute x12, starting transfers between devices, swap(): return lax.ppermute(value, axis, [(0, 1), (1, 0)])  22.1 us
  transfers between devices with their start and end apart: 16, of which 8 were waited for; matrix products, arithmetic and copies ran while one was open for 2% of the time, Pallas kernels for 17%

profile of v1, /device:TPU:1, one launch (start us, length us, event | category | flops | bytes accessed | tf_op | source)
XLA Modules:
  0.0 374.8 jit_solution(10218681548150153807)
XLA Ops:
  7.2 0.0 all-gather.5.cloned.1.call-start
  7.2 0.6 stack.23.ids
  7.8 3.3 pack.1
  11.1 36.2 %all_to_all.5.own = f32[8,2,128,128]{3,2,1,0:T(8,128)S(1)} all-to-all(f32[8,2,128,128]{3,2,1,0:T(8,128)} %bitcast.10), channel_id=1, replica_groups=mesh['x'=4,'yh'=2,'yl'=2,'core'=2,'front'=8] {'front'}, dimensions={0} | all-to-all | bytes 2097152 | tf_op jit(solution)/shard_map/all_to_all | solution.py:409
  47.4 2.5 collective-permute-start
  49.8 2.3 collective-permute-done.other
  52.1 1.0 copy-done.9
  53.1 4.5 %assemble.1 = (f32[4,128,128]{2,1,0:T(8,128)}, f32[4,128,128]{2,1,0:T(8,128)}, f32[4,128,128]{2,1,0:T(8,128)}) custom-call(s32[5]{0:T(128)} %stack.23.ids, s32[16,2,16]{2,1,0:T(2,128)} %map_one.3, s32[16,16,16]{2,1,0:T(8,128)} %pattern_one.1, f32[8,2,128,128]{3,2,1,0:T(8,128)} %copy-done.2, f32[8,2,128,128]{3,2,1,0:T(8,128)} %copy-done.9, f32[1024,256]{1,0:T(8,128)} %initial.1), custom_call_target="tpu_custom_call" | custom-call | tf_op jit(solution)/shard_map/assemble/pallas_call | solution.py:373
  57.6 0.0 all-gather.5.cloned.1.call-update
  57.6 0.0 all-gather.7.cloned.1.call-start
  57.7 0.7 all-gather.7.cloned.1.call-update
  58.4 0.0 all-gather.9.cloned.1.call-start
  58.4 0.7 all-gather.9.cloned.1.call-update
  59.1 0.0 all-gather.11.cloned.1.call-start
  59.2 0.5 all-gather.11.cloned.1.call-update
  59.7 31.5 %all-gather.5.cloned.1.call-done.own = f32[8,512,128]{2,1,0:T(8,128)} async-done(((f32[1,512,128]{2,1,0:T(8,128)}), f32[8,512,128]{2,1,0:T(8,128)}) %all-gather.5.cloned.1.call-update) | async-done | bytes 2097168 | tf_op jit(solution)/shard_map/all_gather | solution.py:422
  91.2 4.4 %collective-permute-start.1 = (f32[8,512,128]{2,1,0:T(8,128)}, f32[8,512,128]{2,1,0:T(8,128)}, u32[]{:S(2)}, u32[]{:S(2)}) collective-permute-start(f32[8,512,128]{2,1,0:T(8,128)} %all-gather.5.cloned.1.call-done.own), channel_id=1, source_target_pairs={{0,8},{8,0},{1,9},{9,1},{2,10},{10,2},{3,11},{11,3},{4,12},{12,4},... | collective-permute-start | bytes 6291464 | tf_op jit(solution)/shard_map/ppermute | solution.py:385
  95.6 37.1 %all-gather.7.cloned.1.call-done.lower_own = f32[8,512,128]{2,1,0:T(8,128)} async-done(((f32[1,512,128]{2,1,0:T(8,128)}), f32[8,512,128]{2,1,0:T(8,128)}) %all-gather.7.cloned.1.call-update) | async-done | bytes 2097168 | tf_op jit(solution)/shard_map/all_gather | solution.py:422
  132.7 4.4 %collective-permute-start.2 = (f32[8,512,128]{2,1,0:T(8,128)}, f32[8,512,128]{2,1,0:T(8,128)S(1)}, u32[]{:S(2)}, u32[]{:S(2)}) collective-permute-start(f32[8,512,128]{2,1,0:T(8,128)} %all-gather.7.cloned.1.call-done.lower_own), channel_id=1, source_target_pairs={{0,8},{8,0},{1,9},{9,1},{2,10},{10,2},{3,11},{11,3},{4,12},{12,4},... | collective-permute-start | bytes 6291464 | tf_op jit(solution)/shard_map/ppermute | solution.py:385
  137.1 37.1 %all-gather.9.cloned.1.call-done.trail_own = f32[8,512,128]{2,1,0:T(8,128)} async-done(((f32[1,512,128]{2,1,0:T(8,128)}), f32[8,512,128]{2,1,0:T(8,128)}) %all-gather.9.cloned.1.call-update) | async-done | bytes 2097168 | tf_op jit(solution)/shard_map/all_gather | solution.py:422
  174.2 4.4 %collective-permute-start.3 = (f32[8,512,128]{2,1,0:T(8,128)}, f32[8,512,128]{2,1,0:T(8,128)}, u32[]{:S(2)}, u32[]{:S(2)}) collective-permute-start(f32[8,512,128]{2,1,0:T(8,128)} %all-gather.9.cloned.1.call-done.trail_own), channel_id=1, source_target_pairs={{0,8},{8,0},{1,9},{9,1},{2,10},{10,2},{3,11},{11,3},{4,12},{12,4},... | collective-permute-start | bytes 6291464 | tf_op jit(solution)/shard_map/ppermute | solution.py:385
  178.6 0.0 collective-permute-done.1.other
  178.6 41.8 %chol.1 = (f32[8,1024,128]{2,1,0:T(8,128)}, f32[8,128,128]{2,1,0:T(8,128)}) custom-call(s32[5]{0:T(128)} %stack.23.ids, f32[8,512,128]{2,1,0:T(8,128)} %all-gather.5.cloned.1.call-done.own, f32[8,512,128]{2,1,0:T(8,128)} %collective-permute-done.1.other), custom_call_target="tpu_custom_call" | custom-call | tf_op jit(solution)/shard_map/chol/pallas_call | solution.py:373
  220.4 0.0 collective-permute-done.2.lower_other
  220.4 0.0 collective-permute-done.3.trail_other
  220.4 1.3 copy-done.3
  221.6 20.6 %rest.1 = (f32[1024,128]{1,0:T(8,128)}, f32[36,128,128]{2,1,0:T(8,128)}) custom-call(s32[5]{0:T(128)} %stack.23.ids, f32[8,1024,128]{2,1,0:T(8,128)} %get-tuple-element.18.chol, f32[8,128,128]{2,1,0:T(8,128)} %get-tuple-element.19.inverse, f32[8,512,128]{2,1,0:T(8,128)} %all-gather.7.cloned.1.call-done.lower_own, f32[8,512,128]{2,1,0:T(8,128)} %copy-done.3, ...), custom_call_target="tpu_custom_call" | custom-call | tf_op jit(solution)/shard_map/rest/pallas_call | solution.py:373
  242.2 2.9 slice_select_fusion
  245.1 1.2 collective-permute-start.10
  246.3 2.7 fusion
  249.1 0.5 collective-permute-start.4
  249.5 23.2 %collective-permute-done.10.child_far_own = f32[18,128,128]{2,1,0:T(8,128)S(1)} collective-permute-done((f32[18,128,128]{2,1,0:T(8,128)S(1)}, f32[18,128,128]{2,1,0:T(8,128)S(1)}, u32[]{:S(2)}, u32[]{:S(2)}) %collective-permute-start.10) | collective-permute-done | bytes 1179680 | tf_op jit(solution)/shard_map/ppermute | solution.py:385
  272.7 1.2 collective-permute-start.11
  273.9 0.0 collective-permute-start.5
  273.9 21.3 %collective-permute-done.4.corner_yl = f32[8,256,128]{2,1,0:T(8,128)S(1)} collective-permute-done((f32[8,256,128]{2,1,0:T(8,128)S(1)}, f32[8,256,128]{2,1,0:T(8,128)S(1)}, u32[]{:S(2)}, u32[]{:S(2)}) %collective-permute-start.4) | collective-permute-done | bytes 1048608 | tf_op jit(solution)/shard_map/ppermute | solution.py:385
  295.2 1.2 collective-permute-start.6
  296.4 1.2 collective-permute-start.7
  297.7 0.4 collective-permute-start.8
  298.0 3.5 collective-permute-done.7.row_yl
  301.5 0.9 collective-permute-start.9
  302.4 0.0 collective-permute-done.8.row_core
  302.4 1.0 collective-permute-done.9.row_both
  303.4 0.0 collective-permute-done.5.corner_core
  303.4 0.0 collective-permute-done.11.child_far_other
  303.4 1.0 copy-done.8
  304.4 0.4 copy-done.7
  304.8 0.6 copy-done.5
  305.4 62.5 %second.1 = (f32[512,128]{1,0:T(8,128)}, f32[256,128]{1,0:T(8,128)}) custom-call(s32[5]{0:T(128)} %stack.23.ids, s32[8,2,16]{2,1,0:T(2,128)} %map_two.1, f32[8,256,128]{2,1,0:T(8,128)} %copy-done.1, f32[8,256,128]{2,1,0:T(8,128)} %copy-done.6, f32[8,256,128]{2,1,0:T(8,128)} %copy-done.7, f32[8,256,128]{2,1,0:T(8,128)} %copy-done.8, ...), custom_call_target="tpu_custom_call" | custom-call | tf_op jit(solution)/shard_map/second/pallas_call | solution.py:373
  (25 shorter events, 0.0 us)
Async XLA Ops:
  7.2 84.0 %all-gather.5.cloned.1.call-start = ((), (), s32[]{:S(2)}) async-start(), calls=%async_computation.1 | async-start | bytes 2359296 | tf_op jit(solution)/shard_map/all_gather | solution.py:422
  47.4 4.7 %copy-start.2 = (f32[8,2,128,128]{3,2,1,0:T(8,128)}, f32[8,2,128,128]{3,2,1,0:T(8,128)S(1)}, u32[]{:S(2)}) copy-start(f32[8,2,128,128]{3,2,1,0:T(8,128)S(1)} %all_to_all.5.own) | copy-start | bytes 3145732
  47.4 4.7 %collective-permute-start = (f32[8,2,128,128]{3,2,1,0:T(8,128)S(1)}, f32[8,2,128,128]{3,2,1,0:T(8,128)S(1)}, u32[]{:S(2)}, u32[]{:S(2)}) collective-permute-start(f32[8,2,128,128]{3,2,1,0:T(8,128)S(1)} %all_to_all.5.own), channel_id=1, source_target_pairs={{0,8},{8,0},{1,9},{9,1},{2,10},{10,2},{3,11},{11,3},{4,12},{12,4},... | collective-permute-start | bytes 3145736 | tf_op jit(solution)/shard_map/ppermute | solution.py:385
  52.1 1.0 copy-start.9
  57.6 75.1 %all-gather.7.cloned.1.call-start = ((), (), s32[]{:S(2)}) async-start(), calls=%async_computation.2 | async-start | bytes 2359296 | tf_op jit(solution)/shard_map/all_gather | solution.py:422
  58.4 115.8 %all-gather.9.cloned.1.call-start = ((), (), s32[]{:S(2)}) async-start(), calls=%async_computation.3 | async-start | bytes 2359296 | tf_op jit(solution)/shard_map/all_gather | solution.py:422
  59.1 187.2 %all-gather.11.cloned.1.call-start = ((), (), s32[]{:S(2)}) async-start(), calls=%async_computation.4 | async-start | bytes 2359296 | tf_op jit(solution)/shard_map/all_gather | solution.py:422
  91.2 87.3 %collective-permute-start.1 = (f32[8,512,128]{2,1,0:T(8,128)}, f32[8,512,128]{2,1,0:T(8,128)}, u32[]{:S(2)}, u32[]{:S(2)}) collective-permute-start(f32[8,512,128]{2,1,0:T(8,128)} %all-gather.5.cloned.1.call-done.own), channel_id=1, source_target_pairs={{0,8},{8,0},{1,9},{9,1},{2,10},{10,2},{3,11},{11,3},{4,12},{12,4},... | collective-permute-start | bytes 6291464 | tf_op jit(solution)/shard_map/ppermute | solution.py:385
  132.7 87.7 %collective-permute-start.2 = (f32[8,512,128]{2,1,0:T(8,128)}, f32[8,512,128]{2,1,0:T(8,128)S(1)}, u32[]{:S(2)}, u32[]{:S(2)}) collective-permute-start(f32[8,512,128]{2,1,0:T(8,128)} %all-gather.7.cloned.1.call-done.lower_own), channel_id=1, source_target_pairs={{0,8},{8,0},{1,9},{9,1},{2,10},{10,2},{3,11},{11,3},{4,12},{12,4},... | collective-permute-start | bytes 6291464 | tf_op jit(solution)/shard_map/ppermute | solution.py:385
  174.2 46.2 %collective-permute-start.3 = (f32[8,512,128]{2,1,0:T(8,128)}, f32[8,512,128]{2,1,0:T(8,128)}, u32[]{:S(2)}, u32[]{:S(2)}) collective-permute-start(f32[8,512,128]{2,1,0:T(8,128)} %all-gather.9.cloned.1.call-done.trail_own), channel_id=1, source_target_pairs={{0,8},{8,0},{1,9},{9,1},{2,10},{10,2},{3,11},{11,3},{4,12},{12,4},... | collective-permute-start | bytes 6291464 | tf_op jit(solution)/shard_map/ppermute | solution.py:385
  220.4 1.3 copy-start.3
  245.1 3.9 %copy-start = (f32[18,128,128]{2,1,0:T(8,128)}, f32[18,128,128]{2,1,0:T(8,128)S(1)}, u32[]{:S(2)}) copy-start(f32[18,128,128]{2,1,0:T(8,128)S(1)} %get-tuple-element.30.child_half_own) | copy-start | bytes 3538948
  245.1 51.3 %copy-start.10 = (f32[2,128,128]{2,1,0:T(8,128)S(1)}, f32[2,128,128]{2,1,0:T(8,128)}, u32[]{:S(2)}) copy-start(f32[2,128,128]{2,1,0:T(8,128)} %get-tuple-element.24.row_own) | copy-start | bytes 393220
  245.1 27.6 %collective-permute-start.10 = (f32[18,128,128]{2,1,0:T(8,128)S(1)}, f32[18,128,128]{2,1,0:T(8,128)S(1)}, u32[]{:S(2)}, u32[]{:S(2)}) collective-permute-start(f32[18,128,128]{2,1,0:T(8,128)S(1)} %get-tuple-element.30.child_half_own), channel_id=1, source_target_pairs={{0,16},{16,0},{1,17},{17,1},{2,18},{18,2},{3,19},{19,3},{4,20},{20... | collective-permute-start | bytes 3538952 | tf_op jit(solution)/shard_map/ppermute | solution.py:385
  249.1 55.3 %copy-start.1 = (f32[8,256,128]{2,1,0:T(8,128)}, f32[8,256,128]{2,1,0:T(8,128)S(1)}, u32[]{:S(2)}) copy-start(f32[8,256,128]{2,1,0:T(8,128)S(1)} %get-tuple-element.32.corner_own) | copy-start | bytes 3145732
  249.1 46.1 %collective-permute-start.4 = (f32[8,256,128]{2,1,0:T(8,128)S(1)}, f32[8,256,128]{2,1,0:T(8,128)S(1)}, u32[]{:S(2)}, u32[]{:S(2)}) collective-permute-start(f32[8,256,128]{2,1,0:T(8,128)S(1)} %get-tuple-element.32.corner_own), channel_id=1, source_target_pairs={{0,16},{16,0},{1,17},{17,1},{2,18},{18,2},{3,19},{19,3},{4,20},{20... | collective-permute-start | bytes 3145736 | tf_op jit(solution)/shard_map/ppermute | solution.py:385
  272.7 31.6 %copy-start.4 = (f32[18,128,128]{2,1,0:T(8,128)}, f32[18,128,128]{2,1,0:T(8,128)S(1)}, u32[]{:S(2)}) copy-start(f32[18,128,128]{2,1,0:T(8,128)S(1)} %collective-permute-done.10.child_far_own) | copy-start | bytes 3538948
  272.7 30.7 %collective-permute-start.11 = (f32[18,128,128]{2,1,0:T(8,128)S(1)}, f32[18,128,128]{2,1,0:T(8,128)S(1)}, u32[]{:S(2)}, u32[]{:S(2)}) collective-permute-start(f32[18,128,128]{2,1,0:T(8,128)S(1)} %collective-permute-done.10.child_far_own), channel_id=1, source_target_pairs={{0,8},{8,0},{1,9},{9,1},{2,10},{10,2},{3,11},{11,3},{4,12},{12,4},... | collective-permute-start | bytes 3538952 | tf_op jit(solution)/shard_map/ppermute | solution.py:385
  273.9 29.5 %collective-permute-start.5 = (f32[8,256,128]{2,1,0:T(8,128)S(1)}, f32[8,256,128]{2,1,0:T(8,128)S(1)}, u32[]{:S(2)}, u32[]{:S(2)}) collective-permute-start(f32[8,256,128]{2,1,0:T(8,128)S(1)} %get-tuple-element.32.corner_own), channel_id=1, source_target_pairs={{0,8},{8,0},{1,9},{9,1},{2,10},{10,2},{3,11},{11,3},{4,12},{12,4},... | collective-permute-start | bytes 3145736 | tf_op jit(solution)/shard_map/ppermute | solution.py:385
  295.2 9.2 %copy-start.6 = (f32[8,256,128]{2,1,0:T(8,128)}, f32[8,256,128]{2,1,0:T(8,128)S(1)}, u32[]{:S(2)}) copy-start(f32[8,256,128]{2,1,0:T(8,128)S(1)} %collective-permute-done.4.corner_yl) | copy-start | bytes 3145732
  295.2 8.2 %collective-permute-start.6 = (f32[8,256,128]{2,1,0:T(8,128)S(1)}, f32[8,256,128]{2,1,0:T(8,128)S(1)}, u32[]{:S(2)}, u32[]{:S(2)}) collective-permute-start(f32[8,256,128]{2,1,0:T(8,128)S(1)} %collective-permute-done.4.corner_yl), channel_id=1, source_target_pairs={{0,8},{8,0},{1,9},{9,1},{2,10},{10,2},{3,11},{11,3},{4,12},{12,4},... | collective-permute-start | bytes 3145736 | tf_op jit(solution)/shard_map/ppermute | solution.py:385
  296.4 5.1 %collective-permute-start.7 = (f32[2,128,128]{2,1,0:T(8,128)S(1)}, f32[2,128,128]{2,1,0:T(8,128)S(1)}, u32[]{:S(2)}, u32[]{:S(2)}) collective-permute-start(f32[2,128,128]{2,1,0:T(8,128)S(1)} %copy-done.10), channel_id=1, source_target_pairs={{0,16},{16,0},{1,17},{17,1},{2,18},{18,2},{3,19},{19,3},{4,20},{20... | collective-permute-start | bytes 393224 | tf_op jit(solution)/shard_map/ppermute | solution.py:385
  297.7 4.7 %collective-permute-start.8 = (f32[2,128,128]{2,1,0:T(8,128)S(1)}, f32[2,128,128]{2,1,0:T(8,128)S(1)}, u32[]{:S(2)}, u32[]{:S(2)}) collective-permute-start(f32[2,128,128]{2,1,0:T(8,128)S(1)} %copy-done.10), channel_id=1, source_target_pairs={{0,8},{8,0},{1,9},{9,1},{2,10},{10,2},{3,11},{11,3},{4,12},{12,4},... | collective-permute-start | bytes 393224 | tf_op jit(solution)/shard_map/ppermute | solution.py:385
  301.5 2.9 copy-start.11
  301.5 1.9 collective-permute-start.9
  302.4 2.0 copy-start.12
  303.4 1.0 copy-start.13
  303.4 1.4 copy-start.7
  303.4 1.0 copy-start.8
  304.4 1.0 copy-start.5
Sparse Core Ops, SparseCore 0:
  57.7 33.4 all-gather.4
  93.0 39.6 all-gather.6
  134.5 39.6 all-gather.8
  176.4 39.6 all-gather.10
